TPU v7x, 32 devices: a whole 2x2x4 slice. The times are simulated.
32 devices in a mesh: days: 2 (over x), tm: 8 (over z, y), sta: 2 (over core).
Axes of the slice: x: 2, y: 2, z: 4, core: 2. Of those that a mesh axis runs over, the one named last changes fastest.
Arguments:
- records: bfloat16 [2048, 2048], P('sta', ('days', 'tm')), parts along dimension 1, may hold values from -6 to 6
- following: bfloat16 [2048, 510], P('sta', 'days'), parts along dimension 1, may hold values from -6 to 6
- library: bfloat16 [32, 2048, 256], P(None, ('sta', 'tm')), may hold values from -6 to 6
- template_ids: int32 [2, 8], replicated, may hold values from 0 to 31
- channel_mask: int32 [32, 2048], replicated, may hold values 0 or 1
- station_group: int32 [2048], replicated, may hold values from 0 to 127
Outputs:
- detection: float32 [2, 8, 2048], P('sta', None, ('days', 'tm')), parts along dimension 2
There are 2 independent parts, one for each index of `days`. A program takes and returns all parts, laid end to end along the dimension named above; an argument that names none is the same for every part. Nothing has to cross between parts.
All inputs are finite; a program needn't handle non-finite values.
Results may differ from a plain program's by a relative error of at most 0.0003.
Values may be sent and summed in bfloat16 or wider, within the bound.
A program may use at most 128 MiB of HBM per device.

v0:
```python
import jax
import jax.numpy as jnp
from jax import lax
from jax.sharding import PartitionSpec as P

W = 256
NB = 2
KB = 8
G = 128


epsilon = 1e-06


def inverse_norm(stream_rows, out_len):
    squares = jnp.square(stream_rows.astype(jnp.float32))
    running = jnp.cumsum(squares, axis=1)
    running = jnp.concatenate([jnp.zeros((running.shape[0], 1), jnp.float32), running], axis=1)
    energy = (running[:, W : W + out_len] - running[:, :out_len]) / W
    return 1.0 / jnp.sqrt(energy + epsilon)


def correlate(rows, temp_rows, out_len):
    block_size = rows.shape[0]
    slot_count = temp_rows.shape[0]
    kernel = jnp.transpose(temp_rows, (1, 0, 2)).reshape(block_size * slot_count, 1, W)
    result = lax.conv_general_dilated(
        rows[None],
        kernel,
        (1,),
        "VALID",
        dimension_numbers=("NCH", "OIH", "NCH"),
        feature_group_count=block_size,
        preferred_element_type=jnp.float32,
    )
    return result[0, :, :out_len].reshape(block_size, slot_count, out_len)


def station_terms(stream_rows, temps, weights, inverse):
    station_count = stream_rows.shape[0]
    out_len = inverse.shape[1]
    slot_count = temps.shape[0]
    size_limit = max(1, (1 << 22) // (W * out_len))
    block_size = max(
        (
            divisor
            for divisor in range(1, station_count + 1)
            if station_count % divisor == 0 and divisor <= size_limit
        )
    )
    turn_count = station_count // block_size
    rows_blocks = stream_rows.reshape(turn_count, block_size, stream_rows.shape[1])
    temp_blocks = jnp.moveaxis(temps.reshape(slot_count, turn_count, block_size, W), 1, 0)
    weight_blocks = jnp.moveaxis(weights.reshape(slot_count, turn_count, block_size), 1, 0)
    scale_blocks = inverse.reshape(turn_count, block_size, out_len)

    def advance(running, inputs):
        rows, temp_rows, weight, scale = inputs
        corr = correlate(rows, temp_rows, out_len)
        factor = jnp.transpose(weight)[:, :, None] * scale[:, None, :]
        return (running + jnp.sum(corr * factor, axis=0), None)

    start_zero = jnp.zeros((slot_count, out_len), jnp.float32)
    return lax.scan(advance, start_zero, (rows_blocks, temp_blocks, weight_blocks, scale_blocks))[0]


def shards(records, following, library, template_ids, channel_mask, station_group):
    sta_rows = records.shape[0]
    block_len = records.shape[1]
    sub_rows = library.shape[1]
    base = lax.axis_index("sta") * sta_rows
    onehot = (station_group[:, None] == jnp.arange(G, dtype=jnp.int32)[None, :]).astype(jnp.int32)
    counts = jnp.dot(channel_mask, onehot, preferred_element_type=jnp.int32)
    my_mask = lax.dynamic_slice_in_dim(channel_mask, base, sta_rows, 1)
    my_group = lax.dynamic_slice_in_dim(station_group, base, sta_rows, 0)
    per_station = jnp.take(counts, my_group, axis=1)
    scaled = my_mask.astype(jnp.float32) / jnp.sqrt(
        jnp.float32(W * G) * jnp.maximum(per_station, 1).astype(jnp.float32)
    )
    flat_ids = template_ids.reshape(-1)
    position = lax.axis_index("tm")
    moved = lax.all_to_all(records, "tm", split_axis=0, concat_axis=1, tiled=True)
    offset = position * sub_rows
    tail_rows = lax.dynamic_slice_in_dim(following, offset, sub_rows, 0)
    stream = jnp.concatenate([moved, tail_rows], axis=1)
    inverse = inverse_norm(stream, moved.shape[1])
    tmean = jnp.mean(jnp.square(library.astype(jnp.float32)), axis=2)
    factor = lax.dynamic_slice_in_dim(scaled, offset, sub_rows, 1) / jnp.sqrt(tmean + epsilon)
    chosen = jnp.take(library, flat_ids, axis=0)
    weights = jnp.take(factor, flat_ids, axis=0)
    partial_sum = station_terms(stream, chosen, weights, inverse)
    totals = lax.psum_scatter(partial_sum, "tm", scatter_dimension=1, tiled=True)
    return lax.psum_scatter(
        totals.reshape(NB, KB, block_len), "sta", scatter_dimension=0, tiled=True
    )


def solution(mesh):
    placed = (
        P("sta", ("days", "tm")),
        P("sta", "days"),
        P(None, ("sta", "tm"), None),
        P(),
        P(),
        P(),
    )
    return jax.shard_map(
        shards,
        mesh=mesh,
        in_specs=placed,
        out_specs=P("sta", None, ("days", "tm")),
        check_vma=False,
    )
```

profile of v0, /device:TPU:0, one launch (start us, length us, event | category | flops | bytes accessed | tf_op | source)
XLA Modules:
  0.0 272.6 jit_solution(17316995010624979843)
XLA Ops:
  6.5 7.6 %all-to-all-start = ((bf16[8,128,128]{2,1,0:T(8,128)(2,1)}), bf16[8,128,128]{2,1,0:T(8,128)(2,1)S(1)}, u32[]{:S(2)}, u32[]{:S(2)}) async-start(bf16[8,128,128]{2,1,0:T(8,128)(2,1)} %bitcast.60), calls=%async_computation | async-start | bytes 524288 | tf_op jit(solution)/shard_map/all_to_all | solution.py:82
  14.2 0.7 fusion.14
  14.9 0.7 compare_and_fusion
  15.6 0.8 reshape.93
  16.3 0.8 reshape.92
  17.1 0.7 copy.50
  17.8 1.6 convolution_bitcast_fusion
  19.5 2.8 %gather_fusion.1 = s32[1024,32]{1,0:T(8,128)S(1)} fusion(s32[32,128]{0,1:T(8,128)S(1)} %copy.46, s32[1024]{0:T(1024)S(1)} %fusion.14), kind=kCustom, calls=%fused_computation.1 | custom fusion | bytes 266240 | tf_op jit(solution)/shard_map/jit(_take)/gather | solution.py:76
  22.4 0.8 copy.47
  23.2 0.6 multiply_reduce_fusion.1
  23.8 1.6 gather_fusion
  25.5 0.7 fusion.13
  26.3 0.6 gather_fusion.2
  27.0 2.4 select_bitcast_fusion
  29.8 0.4 fusion.6
  30.4 0.2 copy.52
  30.8 0.2 copy.53
  31.2 0.8 pad_maximum_fusion
  32.0 173.0 %while.11 = (s32[]{:T(128)}, f32[16,1024]{1,0:T(8,128)S(1)}, bf16[8,16,1279]{2,1,0:T(8,128)(2,1)}, bf16[8,16,16,256]{3,2,0,1:T(8,128)(2,1)}, f32[8,16,16]{1,2,0:...) while((s32[]{:T(128)}, f32[16,1024]{1,0:T(8,128)S(1)}, ...), condition=%wide.region_5.6_spmd.clone, body=%wide.region_3.5_spmd.clone.sunk | while | flops 2150383616 | bytes 5779415 | solution.py:64
  32.0 0.8 constant_dynamic-slice_fusion.6
  32.8 0.7 copy.65
  33.5 0.9 constant_dynamic-slice_fusion.7
  34.6 17.5 %fusion.23 = f32[1,256,1024]{1,0,2:T(1,128)S(1)} fusion(bf16[1,16,1279]{1,0,2:T(2,128)(2,1)S(1)} %copy.65, s32[256]{0:T(256)S(1)} %get-tuple-element.151, bf16[256,256]{0,1:T(8,128)(2,1)S(1)} %copy.67), kind=kOutput, calls=%fused_computation.5.clone.1 | convolution fusion | flops 2149580800 | bytes 1221600 | tf_op jit(solution)/shard_map/while/body/eval_jaxpr/conv_general_dilated | solution.py:27
  52.0 1.3 copy.68
  53.6 0.8 constant_dynamic-slice_fusion.6
  54.4 0.7 copy.65
  55.1 0.9 constant_dynamic-slice_fusion.7
  56.2 17.5 %fusion.23 = f32[1,256,1024]{1,0,2:T(1,128)S(1)} fusion(bf16[1,16,1279]{1,0,2:T(2,128)(2,1)S(1)} %copy.65, s32[256]{0:T(256)S(1)} %get-tuple-element.151, bf16[256,256]{0,1:T(8,128)(2,1)S(1)} %copy.67), kind=kOutput, calls=%fused_computation.5.clone.1 | convolution fusion | flops 2149580800 | bytes 1221600 | tf_op jit(solution)/shard_map/while/body/eval_jaxpr/conv_general_dilated | solution.py:27
  73.7 1.3 copy.68
  75.2 0.8 constant_dynamic-slice_fusion.6
  76.0 0.7 copy.65
  76.7 0.9 constant_dynamic-slice_fusion.7
  77.8 17.5 %fusion.23 = f32[1,256,1024]{1,0,2:T(1,128)S(1)} fusion(bf16[1,16,1279]{1,0,2:T(2,128)(2,1)S(1)} %copy.65, s32[256]{0:T(256)S(1)} %get-tuple-element.151, bf16[256,256]{0,1:T(8,128)(2,1)S(1)} %copy.67), kind=kOutput, calls=%fused_computation.5.clone.1 | convolution fusion | flops 2149580800 | bytes 1221600 | tf_op jit(solution)/shard_map/while/body/eval_jaxpr/conv_general_dilated | solution.py:27
  95.3 1.3 copy.68
  96.9 0.8 constant_dynamic-slice_fusion.6
  97.6 0.7 copy.65
  98.4 0.9 constant_dynamic-slice_fusion.7
  99.4 17.5 %fusion.23 = f32[1,256,1024]{1,0,2:T(1,128)S(1)} fusion(bf16[1,16,1279]{1,0,2:T(2,128)(2,1)S(1)} %copy.65, s32[256]{0:T(256)S(1)} %get-tuple-element.151, bf16[256,256]{0,1:T(8,128)(2,1)S(1)} %copy.67), kind=kOutput, calls=%fused_computation.5.clone.1 | convolution fusion | flops 2149580800 | bytes 1221600 | tf_op jit(solution)/shard_map/while/body/eval_jaxpr/conv_general_dilated | solution.py:27
  116.9 1.3 copy.68
  118.5 0.8 constant_dynamic-slice_fusion.6
  119.3 0.7 copy.65
  120.0 0.9 constant_dynamic-slice_fusion.7
  121.1 17.5 %fusion.23 = f32[1,256,1024]{1,0,2:T(1,128)S(1)} fusion(bf16[1,16,1279]{1,0,2:T(2,128)(2,1)S(1)} %copy.65, s32[256]{0:T(256)S(1)} %get-tuple-element.151, bf16[256,256]{0,1:T(8,128)(2,1)S(1)} %copy.67), kind=kOutput, calls=%fused_computation.5.clone.1 | convolution fusion | flops 2149580800 | bytes 1221600 | tf_op jit(solution)/shard_map/while/body/eval_jaxpr/conv_general_dilated | solution.py:27
  138.5 1.3 copy.68
  140.1 0.8 constant_dynamic-slice_fusion.6
  140.9 0.7 copy.65
  141.6 0.9 constant_dynamic-slice_fusion.7
  142.7 17.5 %fusion.23 = f32[1,256,1024]{1,0,2:T(1,128)S(1)} fusion(bf16[1,16,1279]{1,0,2:T(2,128)(2,1)S(1)} %copy.65, s32[256]{0:T(256)S(1)} %get-tuple-element.151, bf16[256,256]{0,1:T(8,128)(2,1)S(1)} %copy.67), kind=kOutput, calls=%fused_computation.5.clone.1 | convolution fusion | flops 2149580800 | bytes 1221600 | tf_op jit(solution)/shard_map/while/body/eval_jaxpr/conv_general_dilated | solution.py:27
  160.1 1.3 copy.68
  161.7 0.8 constant_dynamic-slice_fusion.6
  162.5 0.7 copy.65
  163.2 0.9 constant_dynamic-slice_fusion.7
  164.3 17.5 %fusion.23 = f32[1,256,1024]{1,0,2:T(1,128)S(1)} fusion(bf16[1,16,1279]{1,0,2:T(2,128)(2,1)S(1)} %copy.65, s32[256]{0:T(256)S(1)} %get-tuple-element.151, bf16[256,256]{0,1:T(8,128)(2,1)S(1)} %copy.67), kind=kOutput, calls=%fused_computation.5.clone.1 | convolution fusion | flops 2149580800 | bytes 1221600 | tf_op jit(solution)/shard_map/while/body/eval_jaxpr/conv_general_dilated | solution.py:27
  181.8 1.3 copy.68
  183.4 0.8 constant_dynamic-slice_fusion.6
  184.1 0.7 copy.65
  184.8 0.9 constant_dynamic-slice_fusion.7
  185.9 17.5 %fusion.23 = f32[1,256,1024]{1,0,2:T(1,128)S(1)} fusion(bf16[1,16,1279]{1,0,2:T(2,128)(2,1)S(1)} %copy.65, s32[256]{0:T(256)S(1)} %get-tuple-element.151, bf16[256,256]{0,1:T(8,128)(2,1)S(1)} %copy.67), kind=kOutput, calls=%fused_computation.5.clone.1 | convolution fusion | flops 2149580800 | bytes 1221600 | tf_op jit(solution)/shard_map/while/body/eval_jaxpr/conv_general_dilated | solution.py:27
  203.4 1.3 copy.68
  205.0 0.6 copy-done.2
  205.6 0.6 dynamic-slice
  206.2 55.7 %reduce-scatter.2.cloned.1.call-done = f32[16,128]{1,0:T(8,128)} async-done(((f32[16,1024]{1,0:T(8,128)}), f32[16,128]{1,0:T(8,128)}) %reduce-scatter.2.cloned.1.call-update) | async-done | bytes 8208 | tf_op jit(solution)/shard_map/reduce_scatter | solution.py:92
  262.0 2.6 all-reduce.2
  264.6 1.2 constant_dynamic-slice_fusion.3
  (86 shorter events, 4.1 us)
Async XLA Ops:
  6.5 10.5 %copy-start = (bf16[1024,255]{1,0:T(8,128)(2,1)S(1)}, bf16[1024,255]{1,0:T(8,128)(2,1)}, u32[]{:S(2)}) copy-start(bf16[1024,255]{1,0:T(8,128)(2,1)} %param.9) | copy-start | bytes 1566724
  6.5 16.6 %copy-start.1 = (bf16[32,128,256]{2,1,0:T(8,128)(2,1)S(1)}, bf16[32,128,256]{2,1,0:T(8,128)(2,1)}, u32[]{:S(2)}) copy-start(bf16[32,128,256]{2,1,0:T(8,128)(2,1)} %param.10) | copy-start | bytes 6291460
  6.5 22.8 %all-to-all-start = ((bf16[8,128,128]{2,1,0:T(8,128)(2,1)}), bf16[8,128,128]{2,1,0:T(8,128)(2,1)S(1)}, u32[]{:S(2)}, u32[]{:S(2)}) async-start(bf16[8,128,128]{2,1,0:T(8,128)(2,1)} %bitcast.60), calls=%async_computation | async-start | bytes 524288 | tf_op jit(solution)/shard_map/all_to_all | solution.py:82
  14.1 247.9 %reduce-scatter.2.cloned.1.call-start = ((), (), s32[]{:S(2)}) async-start(), calls=%async_computation.2 | async-start | bytes 73728 | tf_op jit(solution)/shard_map/reduce_scatter | solution.py:92
  17.1 0.7 copy-start.3
  23.2 2.3 copy-start.5
  25.5 4.2 %copy-start.6 = (bf16[128,255]{0,1:T(8,128)(2,1)S(1)}, bf16[128,255]{0,1:T(8,128)(2,1)}, u32[]{:S(2)}) copy-start(bf16[128,255]{0,1:T(8,128)(2,1)} %copy.50) | copy-start | bytes 195844
  30.4 0.8 copy-start.4
  30.6 1.4 copy-start.8
  32.0 173.6 %copy-start.7 = (u32[32]{0:T(128)S(1)}, u32[32]{0:T(128)}, u32[]{:S(2)}) copy-start(u32[32]{0:T(128)} %constant.105) | copy-start | bytes 388
  205.0 0.6 copy-start.2
Sparse Core Ops, SparseCore 0:
  205.7 56.1 reduce-scatter.1
where the time goes:
time: 274 us; the launch traced here: 273 us
  matrix products  141 us (51%)
  waiting for transfers between devices  55.8 us (20%)
  local copies, waits for them, and re-layouts  42.9 us (16%)
  between operations  13.6 us (5%)
  other arithmetic  8.16 us (3%)
  starting transfers between devices  7.61 us (3%)
    conv_general_dilated x8, matrix products, correlate(): lax.conv_general_dilated(rows[None], kernel, (1,), 'VALID', dimension_num...  140 us
    reduce_scatter x1, waiting for transfers between devices, shards(): lax.psum_scatter(partial_sum, 'tm', scatter_dimension=1, tiled=True)  55.7 us
    dynamic_slice x32, local copies, waits for them, and re-layouts, station_terms(): lax.scan(advance, start_zero, (rows_blocks, temp_blocks, weight_blocks, s...  19.6 us
    conv_general_dilated x8, local copies, waits for them, and re-layouts, correlate(): lax.conv_general_dilated(rows[None], kernel, (1,), 'VALID', dimension_num...  10.6 us
    all_to_all x1, starting transfers between devices, shards(): lax.all_to_all(records, 'tm', split_axis=0, concat_axis=1, tiled=True)  7.57 us
  transfers between devices with their start and end apart: 2, of which 1 were waited for; matrix products, arithmetic and copies ran while one was open for 6% of the time, Pallas kernels for 0%

commit v1 on v0

v1 whole, which is shorter than its diff:
```python
import functools

import jax
import jax.numpy as jnp
from jax import lax
from jax.experimental import pallas as pl
from jax.experimental.pallas import tpu as pltpu
from jax.sharding import PartitionSpec as P

G = 128
LANES = 128
ROWS = 16


epsilon = 1e-06


def correlate_group(chunk, window, stream_ref, temps_ref, weights_ref, out_ref, base, hankel, scale):
    length = chunk + window
    group = stream_ref.shape[0]
    start = pl.multiple_of(pl.program_id(0) * chunk, LANES)
    rows = stream_ref[:, pl.ds(start, length)]

    total = rows * rows
    span = 1
    while span < LANES:
        total = total + pltpu.roll(total, length - span, 1)
        span *= 2
    energy = total[:, :chunk]
    for step in range(1, window // LANES):
        energy = energy + total[:, step * LANES : step * LANES + chunk]
    scale[...] = lax.rsqrt(energy / window + epsilon)

    for shift in range(ROWS):
        moved = rows if shift == 0 else pltpu.roll(rows, length - shift, 1)
        for block in range(length // LANES):
            base[block, pl.ds(shift, group, stride=ROWS), :] = moved[:, block * LANES : (block + 1) * LANES]

    wide = length - LANES
    acc = None
    for s in range(group):
        slot = s % hankel.shape[0]
        shifted = jnp.concatenate(
            [base[block, s * ROWS : (s + 1) * ROWS, :] for block in range(length // LANES)], axis=1
        ).astype(jnp.bfloat16)
        for part in range(LANES // ROWS):
            hankel[slot, part * ROWS : (part + 1) * ROWS, :] = shifted[:, part * ROWS : part * ROWS + wide]
        matrix = jnp.concatenate(
            [hankel[slot, :, step * LANES : step * LANES + chunk] for step in range(window // LANES)], axis=0
        )
        corr = jnp.dot(temps_ref[s], matrix, preferred_element_type=jnp.float32)
        term = corr * scale[s : s + 1, :] * weights_ref[0, :, s : s + 1]
        acc = term if acc is None else acc + term

    @pl.when(pl.program_id(1) == 0)
    def _():
        out_ref[...] = acc

    @pl.when(pl.program_id(1) != 0)
    def _():
        out_ref[...] += acc


def station_sums(stream, temps, weights, out_len):
    stations, slots, window = temps.shape
    group = min(16, stations)
    chunk = min(1024, out_len)
    length = chunk + window
    full = stream.shape[1]
    groups = stations // group
    weights = jnp.transpose(weights.reshape(slots, groups, group), (1, 0, 2))
    return pl.pallas_call(
        functools.partial(correlate_group, chunk, window),
        grid=(out_len // chunk, groups),
        in_specs=[
            pl.BlockSpec((group, full), lambda c, g: (g, 0)),
            pl.BlockSpec((group, slots, window), lambda c, g: (g, 0, 0)),
            pl.BlockSpec((1, slots, group), lambda c, g: (g, 0, 0)),
        ],
        out_specs=pl.BlockSpec((slots, chunk), lambda c, g: (0, c)),
        out_shape=jax.ShapeDtypeStruct((slots, out_len), jnp.float32),
        scratch_shapes=[
            pltpu.VMEM((length // LANES, group * ROWS, LANES), jnp.float32),
            pltpu.VMEM((2, LANES, length - LANES), jnp.bfloat16),
            pltpu.VMEM((group, chunk), jnp.float32),
        ],
        name="station_sums",
    )(stream, temps, weights)


def station_weights(channel_mask, station_group, flat_ids, chosen, first, sub_rows):
    window = chosen.shape[2]
    mask = jnp.take(channel_mask, flat_ids, axis=0)
    mine = lax.dynamic_slice_in_dim(station_group, first, sub_rows, 0)
    same = (station_group[:, None] == mine[None, :]).astype(jnp.bfloat16)
    counts = jnp.dot(mask.astype(jnp.bfloat16), same, preferred_element_type=jnp.float32)
    my_mask = lax.dynamic_slice_in_dim(mask, first, sub_rows, 1).astype(jnp.float32)
    tmean = jnp.mean(jnp.square(chosen.astype(jnp.float32)), axis=2)
    return my_mask / jnp.sqrt(jnp.float32(window * G) * jnp.maximum(counts, 1.0) * (tmean + epsilon))


def shards(records, following, library, template_ids, channel_mask, station_group):
    sta_rows, block_len = records.shape
    sub_rows = library.shape[1]
    batches, per_batch = template_ids.shape
    flat_ids = template_ids.reshape(-1)
    offset = lax.axis_index("tm") * sub_rows
    first = lax.axis_index("sta") * sta_rows + offset
    moved = lax.all_to_all(records, "tm", split_axis=0, concat_axis=1, tiled=True)
    chosen = jnp.take(library, flat_ids, axis=0)
    weights = station_weights(channel_mask, station_group, flat_ids, chosen, first, sub_rows)
    temps = jnp.transpose(chosen, (1, 0, 2))
    tail_rows = lax.dynamic_slice_in_dim(following, offset, sub_rows, 0)
    pad = jnp.zeros((sub_rows, library.shape[2] - tail_rows.shape[1]), records.dtype)
    stream = jnp.concatenate([moved, tail_rows, pad], axis=1).astype(jnp.float32)
    partial_sum = station_sums(stream, temps, weights, moved.shape[1])
    totals = lax.psum_scatter(partial_sum, "tm", scatter_dimension=1, tiled=True)
    return lax.psum_scatter(
        totals.reshape(batches, per_batch, block_len), "sta", scatter_dimension=0, tiled=True
    )


def solution(mesh):
    placed = (
        P("sta", ("days", "tm")),
        P("sta", "days"),
        P(None, ("sta", "tm"), None),
        P(),
        P(),
        P(),
    )
    return jax.shard_map(
        shards,
        mesh=mesh,
        in_specs=placed,
        out_specs=P("sta", None, ("days", "tm")),
        check_vma=False,
    )
```

time: 274 us -> 114 us (0.42)
  matrix products: 141 us -> 1.37 us
  local copies, waits for them, and re-layouts: 42.9 us -> 7.33 us
  Pallas kernels: 0 us -> 21.8 us
  other arithmetic: 8.16 us -> 3.99 us
    conv_general_dilated x8 -> x0, matrix products: 140 us -> none  [correlate(): lax.conv_general_dilated(rows[None], kernel, (1,), 'VALID', dimension_num...]
    pallas_call x0 -> x1, Pallas kernels: none -> 21.8 us  [station_sums(): pl.pallas_call(functools.partial(correlate_group, chunk, window), grid=(o...]
    dynamic_slice x32 -> x1, local copies, waits for them, and re-layouts: 19.6 us -> 0.09 us  [station_weights(): mine = lax.dynamic_slice_in_dim(station_group, first, sub_rows, 0)]
    conv_general_dilated x8 -> x0, local copies, waits for them, and re-layouts: 10.6 us -> none  [correlate(): lax.conv_general_dilated(rows[None], kernel, (1,), 'VALID', dimension_num...]
  transfers between devices with their start and end apart: 2 -> 2, of which waited for: 1 -> 1; matrix products, arithmetic and copies ran while one was open for 6% -> 9% of each run, Pallas kernels for 0% -> 0%
where the time goes in v1:
time: 114 us
  waiting for transfers between devices  55.8 us (49%)
  Pallas kernels  21.8 us (19%)
  between operations  13.5 us (12%)
  starting transfers between devices  7.48 us (7%)
  local copies, waits for them, and re-layouts  7.33 us (6%)
  other arithmetic  3.99 us (4%)
  blocking collectives  2.59 us (2%)
  matrix products  1.37 us (1%)
    reduce_scatter x1, waiting for transfers between devices, shards(): lax.psum_scatter(partial_sum, 'tm', scatter_dimension=1, tiled=True)  55.8 us
    pallas_call x1, Pallas kernels, station_sums(): pl.pallas_call(functools.partial(correlate_group, chunk, window), grid=(o...  21.8 us
    all_to_all x1, starting transfers between devices, shards(): lax.all_to_all(records, 'tm', split_axis=0, concat_axis=1, tiled=True)  7.44 us
    unnamed x1, blocking collectives  2.59 us
  transfers between devices with their start and end apart: 2, of which 1 were waited for; matrix products, arithmetic and copies ran while one was open for 9% of the time, Pallas kernels for 0%

profile of v1, /device:TPU:0, one launch (start us, length us, event | category | flops | bytes accessed | tf_op | source)
XLA Modules:
  0.0 113.9 jit_solution(15704897064662653709)
XLA Ops:
  6.5 0.0 copy-start
  6.5 7.4 %all-to-all-start = ((bf16[8,128,128]{2,1,0:T(8,128)(2,1)}), bf16[8,128,128]{2,1,0:T(8,128)(2,1)S(1)}, u32[]{:S(2)}, u32[]{:S(2)}) async-start(bf16[8,128,128]{2,1,0:T(8,128)(2,1)} %bitcast.17), calls=%async_computation | async-start | bytes 524288 | tf_op jit(solution)/shard_map/all_to_all | solution.py:109
  14.0 0.0 reduce-scatter.2.cloned.1.call-start
  14.0 0.8 reshape.51
  14.8 0.8 reshape.50
  15.6 0.0 copy-start.1
  15.6 1.6 %gather_fusion.1 = s32[16,2048]{1,0:T(8,128)S(1)} fusion(s32[32,2048]{1,0:T(8,128)} %param.10, s32[1024]{0:T(1024)S(1)} %pad_clamp_fusion), kind=kCustom, calls=%fused_computation.1 | custom fusion | bytes 262208 | tf_op jit(solution)/shard_map/jit(_take)/gather | solution.py:93
  17.2 0.0 copy-done
  17.2 0.6 gather_fusion
  17.8 0.7 broadcast_select_fusion
  18.6 0.7 multiply_reduce_fusion
  19.3 0.1 copy.13
  19.3 0.0 copy-done.1
  19.3 0.1 dynamic_slice.11
  19.4 1.4 %fusion.3 = f32[16,128]{1,0:T(8,128)S(1)} fusion(s32[128]{0:T(128)S(1)} %dynamic_slice.11, s32[2048]{0:T(1024)S(1)} %copy-done.1, s32[16,2048]{1,0:T(8,128)} %broadcast_select_fusion, f32[16,128]{1,0:T(8,128)S(1)} %copy.13, s32[]{:T(128)S(6)} %select_n.43), kind=kOutput, calls=%fused_computation.7 | convolution fusion | flops 8697856 | bytes 164356 | tf_op jit(solution)/shard_map/dot_general | solution.py:96
  20.8 0.1 reshape.52
  20.9 0.6 copy.23
  21.5 0.8 constant_dynamic-slice_fusion.1
  22.4 1.6 %fusion.7.temps_ref = bf16[128,16,256]{2,1,0:T(8,128)(2,1)} fusion(bf16[16,128,256]{2,1,0:T(8,128)(2,1)S(1)} %gather_fusion, pred[16]{0:T(512)(128)(4,1)S(1)} %compare_and_fusion), kind=kLoop, calls=%fused_computation.12 | loop fusion | flops 524288 | bytes 2097168 | tf_op jit(solution)/shard_map/jit(_take)/select_n | solution.py:110
  24.0 0.0 copy-start.2
  24.0 0.0 all-to-all-done
  24.1 0.1 concatenate.3
  24.2 0.9 convert_element_type.13.stream_ref
  25.1 21.8 %station_sums.1 = f32[16,1024]{1,0:T(8,128)} custom-call(f32[128,1280]{1,0:T(8,128)} %convert_element_type.13.stream_ref, bf16[128,16,256]{2,1,0:T(8,128)(2,1)} %fusion.7.temps_ref, f32[8,16,16]{2,1,0:T(8,128)} %bitcast.16), custom_call_target="tpu_custom_call" | custom-call | tf_op jit(solution)/shard_map/station_sums/pallas_call | solution.py:72
  46.9 0.0 reduce-scatter.2.cloned.1.call-update
  46.9 0.0 copy-done.2
  46.9 0.6 dynamic-slice
  47.5 55.8 %reduce-scatter.2.cloned.1.call-done = f32[16,128]{1,0:T(8,128)} async-done(((f32[16,1024]{1,0:T(8,128)}), f32[16,128]{1,0:T(8,128)}) %reduce-scatter.2.cloned.1.call-update) | async-done | bytes 8208 | tf_op jit(solution)/shard_map/reduce_scatter | solution.py:117
  103.3 2.6 %all-reduce = f32[2,8,128]{2,1,0:T(8,128)S(1)} all-reduce(f32[2,8,128]{2,1,0:T(8,128)} %bitcast.18), channel_id=3, replica_groups=mesh['days'=2,'tm'=8,'sta'=2] {'sta'}, use_global_device_ids=true, to_apply=%region_2.3.clone | all-reduce | flops 2048 | bytes 16384
  105.9 1.2 %constant_dynamic-slice_fusion = f32[1,8,128]{2,1,0:T(8,128)} fusion(f32[2,8,128]{2,1,0:T(8,128)S(1)} %all-reduce, u32[]{:T(128)} %bitcast.6), kind=kLoop, calls=%fused_computation.22 | loop fusion | bytes 8196
  (5 shorter events, 0.1 us)
Async XLA Ops:
  6.5 10.7 %copy-start = (bf16[32,128,256]{2,1,0:T(8,128)(2,1)S(1)}, bf16[32,128,256]{2,1,0:T(8,128)(2,1)}, u32[]{:S(2)}) copy-start(bf16[32,128,256]{2,1,0:T(8,128)(2,1)} %param.8) | copy-start | bytes 6291460
  6.5 17.5 %all-to-all-start = ((bf16[8,128,128]{2,1,0:T(8,128)(2,1)}), bf16[8,128,128]{2,1,0:T(8,128)(2,1)S(1)}, u32[]{:S(2)}, u32[]{:S(2)}) async-start(bf16[8,128,128]{2,1,0:T(8,128)(2,1)} %bitcast.17), calls=%async_computation | async-start | bytes 524288 | tf_op jit(solution)/shard_map/all_to_all | solution.py:109
  14.0 89.3 %reduce-scatter.2.cloned.1.call-start = ((), (), s32[]{:S(2)}) async-start(), calls=%async_computation.2 | async-start | bytes 73728 | tf_op jit(solution)/shard_map/reduce_scatter | solution.py:117
  15.6 3.8 %copy-start.1 = (s32[2048]{0:T(1024)S(1)}, s32[2048]{0:T(1024)}, u32[]{:S(2)}) copy-start(s32[2048]{0:T(1024)} %param.11) | copy-start | bytes 24580
  24.0 22.9 %copy-start.2 = (u32[32]{0:T(128)S(1)}, u32[32]{0:T(128)}, u32[]{:S(2)}) copy-start(u32[32]{0:T(128)} %constant.60) | copy-start | bytes 388
Sparse Core Ops, SparseCore 0:
  47.0 56.1 reduce-scatter.1

commit v2 on v1

--- a/solution.py
+++ b/solution.py
@@ -52,13 +52,17 @@
         term = corr * scale[s : s + 1, :] * weights_ref[0, :, s : s + 1]
         acc = term if acc is None else acc + term
 
+    parts = [acc[:, block * LANES : (block + 1) * LANES] for block in range(chunk // LANES)]
+
     @pl.when(pl.program_id(1) == 0)
     def _():
-        out_ref[...] = acc
+        for block, part in enumerate(parts):
+            out_ref[block] = part
 
     @pl.when(pl.program_id(1) != 0)
     def _():
-        out_ref[...] += acc
+        for block, part in enumerate(parts):
+            out_ref[block] += part
 
 
 def station_sums(stream, temps, weights, out_len):
@@ -77,8 +81,8 @@
             pl.BlockSpec((group, slots, window), lambda c, g: (g, 0, 0)),
             pl.BlockSpec((1, slots, group), lambda c, g: (g, 0, 0)),
         ],
-        out_specs=pl.BlockSpec((slots, chunk), lambda c, g: (0, c)),
-        out_shape=jax.ShapeDtypeStruct((slots, out_len), jnp.float32),
+        out_specs=pl.BlockSpec((chunk // LANES, slots, LANES), lambda c, g: (c, 0, 0)),
+        out_shape=jax.ShapeDtypeStruct((out_len // LANES, slots, LANES), jnp.float32),
         scratch_shapes=[
             pltpu.VMEM((length // LANES, group * ROWS, LANES), jnp.float32),
             pltpu.VMEM((2, LANES, length - LANES), jnp.bfloat16),
@@ -86,6 +90,114 @@
         ],
         name="station_sums",
     )(stream, temps, weights)
+
+
+def enter(peers):
+    barrier = pltpu.get_barrier_semaphore()
+    for peer in peers:
+        pl.semaphore_signal(barrier, inc=1, device_id=peer, device_id_type=pl.DeviceIdType.MESH)
+    pl.semaphore_wait(barrier, len(peers))
+
+
+def collect_rows(count, records_ref, following_ref, stream_ref, held, tail, own_sem, send_sem, recv_sem):
+    me = lax.axis_index("tm")
+    rows, block_len = held.shape[1:]
+    offset = pl.multiple_of(me * rows, rows)
+    own = pltpu.make_async_copy(records_ref.at[pl.ds(offset, rows), :], held.at[me], own_sem.at[0])
+    after = pltpu.make_async_copy(following_ref.at[pl.ds(offset, rows), :], tail, own_sem.at[1])
+    own.start()
+    after.start()
+    others = [lax.rem(me + step, count) for step in range(1, count)]
+    enter([{"tm": other} for other in others])
+    copies = []
+    for step, other in enumerate(others):
+        copy = pltpu.make_async_remote_copy(
+            src_ref=records_ref.at[pl.ds(pl.multiple_of(other * rows, rows), rows), :],
+            dst_ref=held.at[me],
+            send_sem=send_sem.at[step],
+            recv_sem=recv_sem.at[step],
+            device_id={"tm": other},
+            device_id_type=pl.DeviceIdType.MESH,
+        )
+        copy.start()
+        copies.append(copy)
+    after.wait()
+    out_len = count * block_len
+    stream_ref[:, out_len:] = jnp.zeros((rows, stream_ref.shape[1] - out_len), jnp.float32)
+    stream_ref[:, out_len : out_len + tail.shape[1]] = tail[...].astype(jnp.float32)
+    own.wait()
+    for copy in copies:
+        copy.wait()
+    for block in range(count):
+        stream_ref[:, block * block_len : (block + 1) * block_len] = held[block].astype(jnp.float32)
+
+
+def collect_stream(records, following, count, window):
+    sta_rows, block_len = records.shape
+    rows = sta_rows // count
+    return pl.pallas_call(
+        functools.partial(collect_rows, count),
+        in_specs=[pl.BlockSpec(memory_space=pl.ANY)] * 2,
+        out_specs=pl.BlockSpec(memory_space=pltpu.VMEM),
+        out_shape=jax.ShapeDtypeStruct((rows, count * block_len + window), jnp.float32),
+        scratch_shapes=[
+            pltpu.VMEM((count, rows, block_len), records.dtype),
+            pltpu.VMEM((rows, following.shape[1]), following.dtype),
+            pltpu.SemaphoreType.DMA((2,)),
+            pltpu.SemaphoreType.DMA((count - 1,)),
+            pltpu.SemaphoreType.DMA((count - 1,)),
+        ],
+        compiler_params=pltpu.CompilerParams(collective_id=0, has_side_effects=True),
+        name="collect_stream",
+    )(records, following)
+
+
+def reduce_blocks(parts_ref, out_ref, held, send_sem, recv_sem):
+    blocks, halves = parts_ref.shape[0], parts_ref.shape[1]
+    count = blocks * halves
+    block, half = lax.axis_index("tm"), lax.axis_index("sta")
+    me = block * halves + half
+    others = []
+    for step in range(1, count):
+        other = lax.rem(me + step, count)
+        others.append((other // halves, lax.rem(other, halves)))
+    enter([{"tm": b, "sta": h} for b, h in others])
+    copies = []
+    for step, (b, h) in enumerate(others):
+        copy = pltpu.make_async_remote_copy(
+            src_ref=parts_ref.at[b, h],
+            dst_ref=held.at[step],
+            send_sem=send_sem.at[step],
+            recv_sem=recv_sem.at[step],
+            device_id={"tm": b, "sta": h},
+            device_id_type=pl.DeviceIdType.MESH,
+        )
+        copy.start()
+        copies.append(copy)
+    total = parts_ref[block, half]
+    for step, copy in enumerate(copies):
+        copy.wait_recv()
+        total = total + held[step]
+    out_ref[...] = total
+    for copy in copies:
+        copy.wait_send()
+
+
+def reduce_parts(parts):
+    count = parts.shape[0] * parts.shape[1]
+    return pl.pallas_call(
+        reduce_blocks,
+        in_specs=[pl.BlockSpec(memory_space=pltpu.VMEM)],
+        out_specs=pl.BlockSpec(memory_space=pltpu.VMEM),
+        out_shape=jax.ShapeDtypeStruct(parts.shape[2:], parts.dtype),
+        scratch_shapes=[
+            pltpu.VMEM((count - 1,) + parts.shape[2:], parts.dtype),
+            pltpu.SemaphoreType.DMA((count - 1,)),
+            pltpu.SemaphoreType.DMA((count - 1,)),
+        ],
+        compiler_params=pltpu.CompilerParams(collective_id=1, has_side_effects=True),
+        name="reduce_parts",
+    )(parts)
 
 
 def station_weights(channel_mask, station_group, flat_ids, chosen, first, sub_rows):
@@ -99,25 +211,22 @@
     return my_mask / jnp.sqrt(jnp.float32(window * G) * jnp.maximum(counts, 1.0) * (tmean + epsilon))
 
 
-def shards(records, following, library, template_ids, channel_mask, station_group):
+def shards(blocks, halves, records, following, library, template_ids, channel_mask, station_group):
     sta_rows, block_len = records.shape
-    sub_rows = library.shape[1]
+    sub_rows, window = library.shape[1:]
     batches, per_batch = template_ids.shape
     flat_ids = template_ids.reshape(-1)
-    offset = lax.axis_index("tm") * sub_rows
-    first = lax.axis_index("sta") * sta_rows + offset
-    moved = lax.all_to_all(records, "tm", split_axis=0, concat_axis=1, tiled=True)
+    first = lax.axis_index("sta") * sta_rows + lax.axis_index("tm") * sub_rows
+    stream = collect_stream(records, following, blocks, window)
     chosen = jnp.take(library, flat_ids, axis=0)
     weights = station_weights(channel_mask, station_group, flat_ids, chosen, first, sub_rows)
     temps = jnp.transpose(chosen, (1, 0, 2))
-    tail_rows = lax.dynamic_slice_in_dim(following, offset, sub_rows, 0)
-    pad = jnp.zeros((sub_rows, library.shape[2] - tail_rows.shape[1]), records.dtype)
-    stream = jnp.concatenate([moved, tail_rows, pad], axis=1).astype(jnp.float32)
-    partial_sum = station_sums(stream, temps, weights, moved.shape[1])
-    totals = lax.psum_scatter(partial_sum, "tm", scatter_dimension=1, tiled=True)
-    return lax.psum_scatter(
-        totals.reshape(batches, per_batch, block_len), "sta", scatter_dimension=0, tiled=True
-    )
+    sums = station_sums(stream, temps, weights, blocks * block_len)
+    tiles = block_len // LANES
+    parts = sums.reshape(blocks, tiles, halves, batches // halves * per_batch, LANES)
+    parts = jnp.swapaxes(parts, 1, 2).reshape(blocks, halves, -1, LANES)
+    mine = reduce_parts(parts).reshape(tiles, batches // halves, per_batch, LANES)
+    return jnp.moveaxis(mine, 0, 2).reshape(batches // halves, per_batch, block_len)
 
 
 def solution(mesh):
@@ -130,7 +239,7 @@
         P(),
     )
     return jax.shard_map(
-        shards,
+        functools.partial(shards, mesh.shape["tm"], mesh.shape["sta"]),
         mesh=mesh,
         in_specs=placed,
         out_specs=P("sta", None, ("days", "tm")),

time: 114 us -> 52.8 us (0.46)
  waiting for transfers between devices: 55.8 us -> 0 us
  Pallas kernels: 21.8 us -> 43.3 us
  between operations: 13.5 us -> 0.07 us
  starting transfers between devices: 7.48 us -> 0 us
  blocking collectives: 2.59 us -> 0 us
  local copies, waits for them, and re-layouts: 7.33 us -> 5.55 us
  other arithmetic: 3.99 us -> 2.47 us
    reduce_scatter x1 -> x0, waiting for transfers between devices: 55.8 us -> none  [shards(): lax.psum_scatter(partial_sum, 'tm', scatter_dimension=1, tiled=True)]
    pallas_call x0 -> x2, Pallas kernels: none -> 21.4 us  [the longest x1 11.9 us: collect_stream(): pl.pallas_call(functools.partial(collect_rows, count), in_specs=[pl.Block...]
    all_to_all x1 -> x0, starting transfers between devices: 7.44 us -> none  [shards(): lax.all_to_all(records, 'tm', split_axis=0, concat_axis=1, tiled=True)]
    unnamed x1 -> x0, blocking collectives: 2.59 us -> none
    dynamic_slice x1, local copies, waits for them, and re-layouts: 0.09 us -> 1.42 us  [station_weights(): mine = lax.dynamic_slice_in_dim(station_group, first, sub_rows, 0)]
  transfers between devices with their start and end apart: 2 -> 0, of which waited for: 1 -> 0; matrix products, arithmetic and copies ran while one was open for 9% -> 0% of each run, Pallas kernels for 0% -> 0%
where the time goes in v2:
time: 52.8 us; the launch traced here: 52.5 us
  Pallas kernels  43.3 us (82%)
  local copies, waits for them, and re-layouts  5.55 us (11%)
  other arithmetic  2.47 us (5%)
  matrix products  1.17 us (2%)
    pallas_call x1, Pallas kernels, station_sums(): pl.pallas_call(functools.partial(correlate_group, chunk, window), grid=(o...  21.9 us
    pallas_call x1, Pallas kernels, collect_stream(): pl.pallas_call(functools.partial(collect_rows, count), in_specs=[pl.Block...  11.9 us
    pallas_call x1, Pallas kernels, reduce_parts(): pl.pallas_call(reduce_blocks, in_specs=[pl.BlockSpec(memory_space=pltpu.V...  9.54 us
    select_n x2, other arithmetic, shards(): chosen = jnp.take(library, flat_ids, axis=0)  1.64 us
    dynamic_slice x1, local copies, waits for them, and re-layouts, station_weights(): mine = lax.dynamic_slice_in_dim(station_group, first, sub_rows, 0)  1.42 us
    unnamed x7, local copies, waits for them, and re-layouts  1.28 us
    dot_general x1, matrix products, station_weights(): jnp.dot(mask.astype(jnp.bfloat16), same, preferred_element_type=jnp.float32)  1.17 us

profile of v2, /device:TPU:0, one launch (start us, length us, event | category | flops | bytes accessed | tf_op | source)
XLA Modules:
  0.0 52.5 jit_solution(2836394035860256425)
XLA Ops:
  0.0 0.0 copy-start
  0.0 0.0 copy-start.2
  0.0 0.0 copy-start.1
  0.0 1.4 %dynamic_slice.7 = s32[128]{0:T(128)} dynamic-slice(s32[2048]{0:T(1024)} %param.11, s32[]{:T(128)S(6)} %select_n.39), dynamic_slice_sizes={128} | dynamic-slice | bytes 1028 | tf_op jit(solution)/shard_map/dynamic_slice | solution.py:206
  1.4 0.8 %reshape.45 = s32[16,1]{0,1:T(1,128)S(1)} reshape(s32[2,8]{1,0:T(2,128)} %param.9) | data formatting | bytes 128 | tf_op jit(solution)/shard_map/reshape | solution.py:218
  2.2 0.0 copy-done
  2.2 0.6 %gather_fusion = bf16[16,128,256]{2,1,0:T(8,128)(2,1)S(1)} fusion(bf16[32,128,256]{2,1,0:T(8,128)(2,1)S(1)} %copy-done, s32[1024]{0:T(1024)S(1)} %pad_clamp_fusion), kind=kCustom, calls=%fused_computation | custom fusion | bytes 2097216 | tf_op jit(solution)/shard_map/jit(_take)/gather | solution.py:221
  2.8 0.0 copy-done.2
  2.8 0.1 reshape.44
  2.9 0.7 %multiply_reduce_fusion = f32[16,128]{0,1:T(8,128)S(1)} fusion(bf16[16,128,256]{2,1,0:T(8,128)(2,1)S(1)} %gather_fusion, pred[16]{0:T(512)(128)(4,1)S(1)} %compare_and_fusion), kind=kLoop, calls=%fused_computation.2 | loop fusion | flops 2095104 | bytes 1056784 | tf_op jit(solution)/shard_map/reduce_sum | solution.py:210
  3.7 0.1 copy.10
  3.7 0.0 copy-done.1
  3.7 0.6 %gather_fusion.1 = s32[16,2048]{1,0:T(8,128)S(1)} fusion(s32[32,2048]{1,0:T(8,128)S(1)} %copy-done.1, s32[1024]{0:T(1024)S(1)} %pad_clamp_fusion), kind=kCustom, calls=%fused_computation.1 | custom fusion | bytes 262208 | tf_op jit(solution)/shard_map/jit(_take)/gather | solution.py:205
  4.4 0.1 broadcast_select_fusion
  4.4 1.2 %fusion.3 = f32[16,128]{1,0:T(8,128)S(1)} fusion(s32[128]{0:T(128)} %dynamic_slice.7, s32[2048]{0:T(1024)} %param.11, s32[16,2048]{1,0:T(8,128)S(1)} %broadcast_select_fusion, f32[16,128]{1,0:T(8,128)S(1)} %copy.10, s32[]{:T(128)S(6)} %select_n.39), kind=kOutput, calls=%fused_computation.7 | convolution fusion | flops 8697856 | bytes 164356 | tf_op jit(solution)/shard_map/dot_general | solution.py:208
  5.6 0.1 reshape.46
  5.7 0.6 %copy.18 = f32[16,8,16]{2,0,1:T(8,128)} copy(f32[16,8,16]{2,1,0:T(8,128)S(1)} %reshape.46) | data formatting | bytes 16384 | tf_op jit(solution)/shard_map/reshape | solution.py:75
  6.3 1.6 %fusion.7.temps_ref = bf16[128,16,256]{2,1,0:T(8,128)(2,1)} fusion(bf16[16,128,256]{2,1,0:T(8,128)(2,1)S(1)} %gather_fusion, pred[16]{0:T(512)(128)(4,1)S(1)} %compare_and_fusion), kind=kLoop, calls=%fused_computation.12 | loop fusion | flops 524288 | bytes 2097168 | tf_op jit(solution)/shard_map/jit(_take)/select_n | solution.py:221
  8.0 11.9 %collect_stream.1.stream_ref = f32[128,1280]{1,0:T(8,128)} custom-call(bf16[1024,128]{1,0:T(8,128)(2,1)} %records_ref.1, bf16[1024,255]{1,0:T(8,128)(2,1)} %following_ref.1), custom_call_target="tpu_custom_call" | custom-call | tf_op jit(solution)/shard_map/collect_stream/pallas_call | solution.py:138
  19.9 21.9 %station_sums.1 = f32[8,16,128]{2,1,0:T(8,128)} custom-call(f32[128,1280]{1,0:T(8,128)} %collect_stream.1.stream_ref, bf16[128,16,256]{2,1,0:T(8,128)(2,1)} %fusion.7.temps_ref, f32[8,16,16]{2,1,0:T(8,128)} %bitcast.9), custom_call_target="tpu_custom_call" | custom-call | tf_op jit(solution)/shard_map/station_sums/pallas_call | solution.py:76
  41.7 9.5 %reduce_parts.1 = f32[8,128]{1,0:T(8,128)} custom-call(f32[8,2,8,128]{3,2,1,0:T(8,128)} %bitcast.10), custom_call_target="tpu_custom_call" | custom-call | tf_op jit(solution)/shard_map/reduce_parts/pallas_call | solution.py:188
  51.3 1.3 %copy.20 = f32[1,8,128]{2,1,0:T(8,128)} copy(f32[1,8,128]{2,1,0:T(8,128)} %bitcast.11) | data formatting | bytes 8192
  (3 shorter events, 0.0 us)
Async XLA Ops:
  0.0 2.2 %copy-start = (bf16[32,128,256]{2,1,0:T(8,128)(2,1)S(1)}, bf16[32,128,256]{2,1,0:T(8,128)(2,1)}, u32[]{:S(2)}) copy-start(bf16[32,128,256]{2,1,0:T(8,128)(2,1)} %param.8) | copy-start | bytes 6291460
  0.0 2.8 %copy-start.2 = (s32[2,8]{1,0:T(2,128)S(1)}, s32[2,8]{1,0:T(2,128)}, u32[]{:S(2)}) copy-start(s32[2,8]{1,0:T(2,128)} %param.9) | copy-start | bytes 196
  0.0 3.7 %copy-start.1 = (s32[32,2048]{1,0:T(8,128)S(1)}, s32[32,2048]{1,0:T(8,128)}, u32[]{:S(2)}) copy-start(s32[32,2048]{1,0:T(8,128)} %param.10) | copy-start | bytes 786436

commit v3 on v2

--- a/solution.py
+++ b/solution.py
@@ -37,8 +37,16 @@
             base[block, pl.ds(shift, group, stride=ROWS), :] = moved[:, block * LANES : (block + 1) * LANES]
 
     wide = length - LANES
+    slots, lanes = weights_ref.shape
+    turn = lax.rem(lanes - pl.program_id(1) * group, lanes)
+    weights = pltpu.roll(weights_ref[...], turn, 1)
     acc = None
     for s in range(group):
+        template = [temps_ref[block, s * slots : (s + 1) * slots, :] for block in range(window // LANES)]
+        squares = sum(piece * piece for piece in template)
+        tmean = jnp.sum(squares, axis=1, keepdims=True) / window
+        weight = weights[:, s : s + 1] * lax.rsqrt(tmean + epsilon)
+        template = jnp.concatenate(template, axis=1).astype(jnp.bfloat16)
         slot = s % hankel.shape[0]
         shifted = jnp.concatenate(
             [base[block, s * ROWS : (s + 1) * ROWS, :] for block in range(length // LANES)], axis=1
@@ -48,8 +56,8 @@
         matrix = jnp.concatenate(
             [hankel[slot, :, step * LANES : step * LANES + chunk] for step in range(window // LANES)], axis=0
         )
-        corr = jnp.dot(temps_ref[s], matrix, preferred_element_type=jnp.float32)
-        term = corr * scale[s : s + 1, :] * weights_ref[0, :, s : s + 1]
+        corr = jnp.dot(template, matrix, preferred_element_type=jnp.float32)
+        term = corr * scale[s : s + 1, :] * weight
         acc = term if acc is None else acc + term
 
     parts = [acc[:, block * LANES : (block + 1) * LANES] for block in range(chunk // LANES)]
@@ -66,20 +74,21 @@
 
 
 def station_sums(stream, temps, weights, out_len):
-    stations, slots, window = temps.shape
+    stations = stream.shape[0]
+    slots, lanes = weights.shape
+    window = temps.shape[0] * LANES
     group = min(16, stations)
     chunk = min(1024, out_len)
     length = chunk + window
     full = stream.shape[1]
     groups = stations // group
-    weights = jnp.transpose(weights.reshape(slots, groups, group), (1, 0, 2))
     return pl.pallas_call(
         functools.partial(correlate_group, chunk, window),
         grid=(out_len // chunk, groups),
         in_specs=[
             pl.BlockSpec((group, full), lambda c, g: (g, 0)),
-            pl.BlockSpec((group, slots, window), lambda c, g: (g, 0, 0)),
-            pl.BlockSpec((1, slots, group), lambda c, g: (g, 0, 0)),
+            pl.BlockSpec((window // LANES, group * slots, LANES), lambda c, g: (0, g, 0)),
+            pl.BlockSpec((slots, lanes), lambda c, g: (0, 0)),
         ],
         out_specs=pl.BlockSpec((chunk // LANES, slots, LANES), lambda c, g: (c, 0, 0)),
         out_shape=jax.ShapeDtypeStruct((out_len // LANES, slots, LANES), jnp.float32),
@@ -99,8 +108,13 @@
     pl.semaphore_wait(barrier, len(peers))
 
 
-def collect_rows(count, records_ref, following_ref, stream_ref, held, tail, own_sem, send_sem, recv_sem):
+def collect_rows(
+    count, ids_ref, records_ref, following_ref, library_ref, mask_ref, group_ref,
+    stream_ref, temps_ref, weights_ref, held, tail, templates, own_sem, send_sem, recv_sem,
+):
     me = lax.axis_index("tm")
+    pull = pltpu.make_async_copy(library_ref, templates, own_sem.at[2])
+    pull.start()
     rows, block_len = held.shape[1:]
     offset = pl.multiple_of(me * rows, rows)
     own = pltpu.make_async_copy(records_ref.at[pl.ds(offset, rows), :], held.at[me], own_sem.at[0])
@@ -125,6 +139,39 @@
     out_len = count * block_len
     stream_ref[:, out_len:] = jnp.zeros((rows, stream_ref.shape[1] - out_len), jnp.float32)
     stream_ref[:, out_len : out_len + tail.shape[1]] = tail[...].astype(jnp.float32)
+
+    stations = mask_ref.shape[1]
+    slots, lanes = weights_ref.shape
+    window = templates.shape[2]
+    first = lax.axis_index("sta") * (rows * count) + offset
+    turn = lax.rem(stations - first, stations)
+    mask = jnp.concatenate([mask_ref[pl.ds(ids_ref[j], 1), :] for j in range(slots)], axis=0)
+    mask = mask.astype(jnp.float32)
+    names = group_ref[...]
+    onehot = lax.broadcasted_iota(jnp.int32, (G, stations), 0) == jnp.broadcast_to(names, (G, stations))
+    counts = lax.dot_general(
+        mask.astype(jnp.bfloat16),
+        onehot.astype(jnp.float32).astype(jnp.bfloat16),
+        (((1,), (1,)), ((), ())),
+        preferred_element_type=jnp.float32,
+    )
+    mine = pltpu.roll(jnp.broadcast_to(names, (8, stations)), turn, 1)[:1, :lanes]
+    chosen = lax.broadcasted_iota(jnp.int32, (G, lanes), 0) == jnp.broadcast_to(mine, (G, lanes))
+    chosen = chosen.astype(jnp.float32).astype(jnp.bfloat16)
+    high = jnp.floor(counts / 128.0) * 128.0
+    low = counts - high
+    per_station = jnp.dot(high.astype(jnp.bfloat16), chosen, preferred_element_type=jnp.float32) + jnp.dot(
+        low.astype(jnp.bfloat16), chosen, preferred_element_type=jnp.float32
+    )
+    my_mask = pltpu.roll(mask, turn, 1)[:, :lanes]
+    weights_ref[...] = my_mask * lax.rsqrt(jnp.float32(window * G) * jnp.maximum(per_station, 1.0))
+
+    pull.wait()
+    for j in range(slots):
+        template = templates[ids_ref[j]].astype(jnp.float32)
+        for block in range(window // LANES):
+            temps_ref[block, pl.ds(j, rows, stride=slots), :] = template[:, block * LANES : (block + 1) * LANES]
+
     own.wait()
     for copy in copies:
         copy.wait()
@@ -132,24 +179,33 @@
         stream_ref[:, block * block_len : (block + 1) * block_len] = held[block].astype(jnp.float32)
 
 
-def collect_stream(records, following, count, window):
+def collect_stream(flat_ids, records, following, library, channel_mask, station_group, count):
     sta_rows, block_len = records.shape
-    rows = sta_rows // count
+    rows, window = library.shape[1:]
+    slots = flat_ids.shape[0]
+    lanes = -(-rows // LANES) * LANES
     return pl.pallas_call(
         functools.partial(collect_rows, count),
-        in_specs=[pl.BlockSpec(memory_space=pl.ANY)] * 2,
-        out_specs=pl.BlockSpec(memory_space=pltpu.VMEM),
-        out_shape=jax.ShapeDtypeStruct((rows, count * block_len + window), jnp.float32),
+        in_specs=[pl.BlockSpec(memory_space=pltpu.SMEM)]
+        + [pl.BlockSpec(memory_space=pl.ANY)] * 3
+        + [pl.BlockSpec(memory_space=pltpu.VMEM)] * 2,
+        out_specs=[pl.BlockSpec(memory_space=pltpu.VMEM)] * 3,
+        out_shape=[
+            jax.ShapeDtypeStruct((rows, count * block_len + window), jnp.float32),
+            jax.ShapeDtypeStruct((window // LANES, rows * slots, LANES), jnp.float32),
+            jax.ShapeDtypeStruct((slots, lanes), jnp.float32),
+        ],
         scratch_shapes=[
             pltpu.VMEM((count, rows, block_len), records.dtype),
             pltpu.VMEM((rows, following.shape[1]), following.dtype),
-            pltpu.SemaphoreType.DMA((2,)),
+            pltpu.VMEM(library.shape, library.dtype),
+            pltpu.SemaphoreType.DMA((3,)),
             pltpu.SemaphoreType.DMA((count - 1,)),
             pltpu.SemaphoreType.DMA((count - 1,)),
         ],
         compiler_params=pltpu.CompilerParams(collective_id=0, has_side_effects=True),
         name="collect_stream",
-    )(records, following)
+    )(flat_ids, records, following, library, channel_mask, station_group.reshape(1, -1))
 
 
 def reduce_blocks(parts_ref, out_ref, held, send_sem, recv_sem):
@@ -200,27 +256,12 @@
     )(parts)
 
 
-def station_weights(channel_mask, station_group, flat_ids, chosen, first, sub_rows):
-    window = chosen.shape[2]
-    mask = jnp.take(channel_mask, flat_ids, axis=0)
-    mine = lax.dynamic_slice_in_dim(station_group, first, sub_rows, 0)
-    same = (station_group[:, None] == mine[None, :]).astype(jnp.bfloat16)
-    counts = jnp.dot(mask.astype(jnp.bfloat16), same, preferred_element_type=jnp.float32)
-    my_mask = lax.dynamic_slice_in_dim(mask, first, sub_rows, 1).astype(jnp.float32)
-    tmean = jnp.mean(jnp.square(chosen.astype(jnp.float32)), axis=2)
-    return my_mask / jnp.sqrt(jnp.float32(window * G) * jnp.maximum(counts, 1.0) * (tmean + epsilon))
-
-
 def shards(blocks, halves, records, following, library, template_ids, channel_mask, station_group):
     sta_rows, block_len = records.shape
-    sub_rows, window = library.shape[1:]
     batches, per_batch = template_ids.shape
-    flat_ids = template_ids.reshape(-1)
-    first = lax.axis_index("sta") * sta_rows + lax.axis_index("tm") * sub_rows
-    stream = collect_stream(records, following, blocks, window)
-    chosen = jnp.take(library, flat_ids, axis=0)
-    weights = station_weights(channel_mask, station_group, flat_ids, chosen, first, sub_rows)
-    temps = jnp.transpose(chosen, (1, 0, 2))
+    stream, temps, weights = collect_stream(
+        template_ids.reshape(-1), records, following, library, channel_mask, station_group, blocks
+    )
     sums = station_sums(stream, temps, weights, blocks * block_len)
     tiles = block_len // LANES
     parts = sums.reshape(blocks, tiles, halves, batches // halves * per_batch, LANES)

time: 52.8 us -> 49.7 us (0.941)
  Pallas kernels: 43.3 us -> 46.9 us
  local copies, waits for them, and re-layouts: 5.55 us -> 2.53 us
  other arithmetic: 2.47 us -> 0 us
  matrix products: 1.17 us -> 0 us
    pallas_call x1, Pallas kernels: 21.9 us -> 23.9 us  [station_sums(): pl.pallas_call(functools.partial(correlate_group, chunk, window), grid=(o...]
    select_n x3 -> x0, other arithmetic: 1.72 us -> none  [the longest x2 1.64 us: shards(): chosen = jnp.take(library, flat_ids, axis=0)]
    pallas_call x1, Pallas kernels: 11.9 us -> 13.6 us  [collect_stream(): pl.pallas_call(functools.partial(collect_rows, count), in_specs=[pl.Block...]
    dynamic_slice x1 -> x0, local copies, waits for them, and re-layouts: 1.42 us -> none  [station_weights(): mine = lax.dynamic_slice_in_dim(station_group, first, sub_rows, 0)]
    gather x2 -> x0, local copies, waits for them, and re-layouts: 1.24 us -> none  [the longest x1 0.62 us: station_weights(): mask = jnp.take(channel_mask, flat_ids, axis=0)]
    dot_general x1 -> x0, matrix products: 1.17 us -> none  [station_weights(): jnp.dot(mask.astype(jnp.bfloat16), same, preferred_element_type=jnp.float32)]
    reduce_sum x1 -> x0, other arithmetic: 0.73 us -> none  [station_weights(): tmean = jnp.mean(jnp.square(chosen.astype(jnp.float32)), axis=2)]
    reshape x4 -> x1, local copies, waits for them, and re-layouts: 1.56 us -> 1.27 us  [shards(): template_ids.reshape(-1)]
where the time goes in v3:
time: 49.7 us; the launch traced here: 49.5 us
  Pallas kernels  46.9 us (94%)
  local copies, waits for them, and re-layouts  2.53 us (5%)
    pallas_call x1, Pallas kernels, station_sums(): pl.pallas_call(functools.partial(correlate_group, chunk, window), grid=(o...  23.9 us
    pallas_call x1, Pallas kernels, collect_stream(): pl.pallas_call(functools.partial(collect_rows, count), in_specs=[pl.Block...  13.6 us
    pallas_call x1, Pallas kernels, reduce_parts(): pl.pallas_call(reduce_blocks, in_specs=[pl.BlockSpec(memory_space=pltpu.V...  9.52 us
    reshape x1, local copies, waits for them, and re-layouts, shards(): template_ids.reshape(-1)  1.27 us
    unnamed x1, local copies, waits for them, and re-layouts  1.26 us

profile of v3, /device:TPU:0, one launch (start us, length us, event | category | flops | bytes accessed | tf_op | source)
XLA Modules:
  0.0 49.5 jit_solution(5954729786623417270)
XLA Ops:
  0.0 1.3 %reshape.6.ids_ref = s32[16]{0:T(128)} reshape(s32[2,8]{1,0:T(2,128)} %param.9) | data formatting | bytes 128 | tf_op jit(solution)/shard_map/reshape | solution.py:263
  1.3 13.6 %collect_stream.1 = (f32[128,1280]{1,0:T(8,128)}, f32[2,2048,128]{2,1,0:T(8,128)}, f32[16,128]{1,0:T(8,128)}) custom-call(s32[16]{0:T(128)} %reshape.6.ids_ref, bf16[1024,128]{1,0:T(8,128)(2,1)} %records_ref.1, bf16[1024,255]{1,0:T(8,128)(2,1)} %following_ref.1, bf16[32,128,256]{2,1,0:T(8,128)(2,1)} %library_ref.1, s32[32,2048]{1,0:T(8,128)} %mask_ref.1, ...), custom_call_target="tpu_custom_call" | custom-call | tf_op jit(solution)/shard_map/collect_stream/pallas_call | solution.py:187
  14.9 23.9 %station_sums.1 = f32[8,16,128]{2,1,0:T(8,128)} custom-call(f32[128,1280]{1,0:T(8,128)} %get-tuple-element.8.stream_ref, f32[2,2048,128]{2,1,0:T(8,128)} %get-tuple-element.9.temps_ref, f32[16,128]{1,0:T(8,128)} %get-tuple-element.10.weights_ref), custom_call_target="tpu_custom_call" | custom-call | tf_op jit(solution)/shard_map/station_sums/pallas_call | solution.py:85
  38.7 9.5 %reduce_parts.1 = f32[8,128]{1,0:T(8,128)} custom-call(f32[8,2,8,128]{3,2,1,0:T(8,128)} %bitcast.3), custom_call_target="tpu_custom_call" | custom-call | tf_op jit(solution)/shard_map/reduce_parts/pallas_call | solution.py:244
  48.2 1.3 %copy.8 = f32[1,8,128]{2,1,0:T(8,128)} copy(f32[1,8,128]{2,1,0:T(8,128)} %bitcast.4) | data formatting | bytes 8192

commit v4 on v3

--- a/solution.py
+++ b/solution.py
@@ -31,10 +31,7 @@
         energy = energy + total[:, step * LANES : step * LANES + chunk]
     scale[...] = lax.rsqrt(energy / window + epsilon)
 
-    for shift in range(ROWS):
-        moved = rows if shift == 0 else pltpu.roll(rows, length - shift, 1)
-        for block in range(length // LANES):
-            base[block, pl.ds(shift, group, stride=ROWS), :] = moved[:, block * LANES : (block + 1) * LANES]
+    base[...] = pltpu.roll(rows, length - (ROWS - 1), 1)
 
     wide = length - LANES
     slots, lanes = weights_ref.shape
@@ -48,8 +45,8 @@
         weight = weights[:, s : s + 1] * lax.rsqrt(tmean + epsilon)
         template = jnp.concatenate(template, axis=1).astype(jnp.bfloat16)
         slot = s % hankel.shape[0]
-        shifted = jnp.concatenate(
-            [base[block, s * ROWS : (s + 1) * ROWS, :] for block in range(length // LANES)], axis=1
+        shifted = pltpu.roll(
+            jnp.broadcast_to(base[s : s + 1, :], (ROWS, length)), 0, 1, stride=1, stride_axis=0
         ).astype(jnp.bfloat16)
         for part in range(LANES // ROWS):
             hankel[slot, part * ROWS : (part + 1) * ROWS, :] = shifted[:, part * ROWS : part * ROWS + wide]
@@ -93,7 +90,7 @@
         out_specs=pl.BlockSpec((chunk // LANES, slots, LANES), lambda c, g: (c, 0, 0)),
         out_shape=jax.ShapeDtypeStruct((out_len // LANES, slots, LANES), jnp.float32),
         scratch_shapes=[
-            pltpu.VMEM((length // LANES, group * ROWS, LANES), jnp.float32),
+            pltpu.VMEM((group, length), jnp.float32),
             pltpu.VMEM((2, LANES, length - LANES), jnp.bfloat16),
             pltpu.VMEM((group, chunk), jnp.float32),
         ],
@@ -145,7 +142,8 @@
     window = templates.shape[2]
     first = lax.axis_index("sta") * (rows * count) + offset
     turn = lax.rem(stations - first, stations)
-    mask = jnp.concatenate([mask_ref[pl.ds(ids_ref[j], 1), :] for j in range(slots)], axis=0)
+    ids = [ids_ref[j // ids_ref.shape[1], j % ids_ref.shape[1]] for j in range(slots)]
+    mask = jnp.concatenate([mask_ref[pl.ds(ids[j], 1), :] for j in range(slots)], axis=0)
     mask = mask.astype(jnp.float32)
     names = group_ref[...]
     onehot = lax.broadcasted_iota(jnp.int32, (G, stations), 0) == jnp.broadcast_to(names, (G, stations))
@@ -166,9 +164,12 @@
     my_mask = pltpu.roll(mask, turn, 1)[:, :lanes]
     weights_ref[...] = my_mask * lax.rsqrt(jnp.float32(window * G) * jnp.maximum(per_station, 1.0))
 
+    order = lax.broadcasted_iota(jnp.int32, (window, window), 1) ^ (ROWS - 1)
+    turned = (lax.broadcasted_iota(jnp.int32, (window, window), 0) == order)
+    turned = turned.astype(jnp.float32).astype(jnp.bfloat16)
     pull.wait()
     for j in range(slots):
-        template = templates[ids_ref[j]].astype(jnp.float32)
+        template = jnp.dot(templates[ids[j]], turned, preferred_element_type=jnp.float32)
         for block in range(window // LANES):
             temps_ref[block, pl.ds(j, rows, stride=slots), :] = template[:, block * LANES : (block + 1) * LANES]
 
@@ -179,10 +180,10 @@
         stream_ref[:, block * block_len : (block + 1) * block_len] = held[block].astype(jnp.float32)
 
 
-def collect_stream(flat_ids, records, following, library, channel_mask, station_group, count):
+def collect_stream(template_ids, records, following, library, channel_mask, station_group, count):
     sta_rows, block_len = records.shape
     rows, window = library.shape[1:]
-    slots = flat_ids.shape[0]
+    slots = template_ids.size
     lanes = -(-rows // LANES) * LANES
     return pl.pallas_call(
         functools.partial(collect_rows, count),
@@ -205,7 +206,7 @@
         ],
         compiler_params=pltpu.CompilerParams(collective_id=0, has_side_effects=True),
         name="collect_stream",
-    )(flat_ids, records, following, library, channel_mask, station_group.reshape(1, -1))
+    )(template_ids, records, following, library, channel_mask, station_group.reshape(1, -1))
 
 
 def reduce_blocks(parts_ref, out_ref, held, send_sem, recv_sem):
@@ -260,7 +261,7 @@
     sta_rows, block_len = records.shape
     batches, per_batch = template_ids.shape
     stream, temps, weights = collect_stream(
-        template_ids.reshape(-1), records, following, library, channel_mask, station_group, blocks
+        template_ids, records, following, library, channel_mask, station_group, blocks
     )
     sums = station_sums(stream, temps, weights, blocks * block_len)
     tiles = block_len // LANES

time: 49.7 us -> 51.6 us (1.038)
  Pallas kernels: 46.9 us -> 50.1 us
  local copies, waits for them, and re-layouts: 2.53 us -> 1.26 us
    pallas_call x1, Pallas kernels: 23.9 us -> 27 us  [station_sums(): pl.pallas_call(functools.partial(correlate_group, chunk, window), grid=(o...]
    reshape x1 -> x0, local copies, waits for them, and re-layouts: 1.27 us -> none  [shards(): template_ids.reshape(-1)]
where the time goes in v4:
time: 51.6 us; the launch traced here: 51.4 us
  Pallas kernels  50.1 us (97%)
  local copies, waits for them, and re-layouts  1.26 us (2%)
    pallas_call x1, Pallas kernels, station_sums(): pl.pallas_call(functools.partial(correlate_group, chunk, window), grid=(o...  27 us
    pallas_call x1, Pallas kernels, collect_stream(): pl.pallas_call(functools.partial(collect_rows, count), in_specs=[pl.Block...  13.6 us
    pallas_call x1, Pallas kernels, reduce_parts(): pl.pallas_call(reduce_blocks, in_specs=[pl.BlockSpec(memory_space=pltpu.V...  9.52 us
    unnamed x1, local copies, waits for them, and re-layouts  1.26 us

profile of v4, /device:TPU:0, one launch (start us, length us, event | category | flops | bytes accessed | tf_op | source)
XLA Modules:
  0.0 51.4 jit_solution(17621513232021996228)
XLA Ops:
  0.0 13.6 %collect_stream.1 = (f32[128,1280]{1,0:T(8,128)}, f32[2,2048,128]{2,1,0:T(8,128)}, f32[16,128]{1,0:T(8,128)}) custom-call(s32[2,8]{1,0:T(2,128)} %ids_ref.1, bf16[1024,128]{1,0:T(8,128)(2,1)} %records_ref.1, bf16[1024,255]{1,0:T(8,128)(2,1)} %following_ref.1, bf16[32,128,256]{2,1,0:T(8,128)(2,1)} %library_ref.1, s32[32,2048]{1,0:T(8,128)} %mask_ref.1, ...), custom_call_target="tpu_custom_call" | custom-call | tf_op jit(solution)/shard_map/collect_stream/pallas_call | solution.py:188
  13.6 27.0 %station_sums.1 = f32[8,16,128]{2,1,0:T(8,128)} custom-call(f32[128,1280]{1,0:T(8,128)} %get-tuple-element.8.stream_ref, f32[2,2048,128]{2,1,0:T(8,128)} %get-tuple-element.9.temps_ref, f32[16,128]{1,0:T(8,128)} %get-tuple-element.10.weights_ref), custom_call_target="tpu_custom_call" | custom-call | tf_op jit(solution)/shard_map/station_sums/pallas_call | solution.py:82
  40.6 9.5 %reduce_parts.1 = f32[8,128]{1,0:T(8,128)} custom-call(f32[8,2,8,128]{3,2,1,0:T(8,128)} %bitcast.3), custom_call_target="tpu_custom_call" | custom-call | tf_op jit(solution)/shard_map/reduce_parts/pallas_call | solution.py:245
  50.1 1.3 %copy.8 = f32[1,8,128]{2,1,0:T(8,128)} copy(f32[1,8,128]{2,1,0:T(8,128)} %bitcast.4) | data formatting | bytes 8192

commit v5 on v4

--- a/solution.py
+++ b/solution.py
@@ -15,7 +15,7 @@
 epsilon = 1e-06
 
 
-def correlate_group(chunk, window, stream_ref, temps_ref, weights_ref, out_ref, base, hankel, scale):
+def correlate_group(chunk, window, stream_ref, temps_ref, weights_ref, out_ref, ahead, base, hankel, scale):
     length = chunk + window
     group = stream_ref.shape[0]
     start = pl.multiple_of(pl.program_id(0) * chunk, LANES)
@@ -31,7 +31,17 @@
         energy = energy + total[:, step * LANES : step * LANES + chunk]
     scale[...] = lax.rsqrt(energy / window + epsilon)
 
-    base[...] = pltpu.roll(rows, length - (ROWS - 1), 1)
+    ahead[...] = pltpu.roll(rows, length - (ROWS - 1), 1)
+    batch = min(8, group)
+
+    def turn_rows(step, carry):
+        for k in range(batch):
+            s = step * batch + k
+            row = jnp.broadcast_to(ahead[pl.ds(s, 1), :], (ROWS, length))
+            base[s] = pltpu.roll(row, 0, 1, stride=1, stride_axis=0).astype(base.dtype)
+        return carry
+
+    lax.fori_loop(0, group // batch, turn_rows, 0)
 
     wide = length - LANES
     slots, lanes = weights_ref.shape
@@ -45,9 +55,7 @@
         weight = weights[:, s : s + 1] * lax.rsqrt(tmean + epsilon)
         template = jnp.concatenate(template, axis=1).astype(jnp.bfloat16)
         slot = s % hankel.shape[0]
-        shifted = pltpu.roll(
-            jnp.broadcast_to(base[s : s + 1, :], (ROWS, length)), 0, 1, stride=1, stride_axis=0
-        ).astype(jnp.bfloat16)
+        shifted = base[s].astype(jnp.bfloat16)
         for part in range(LANES // ROWS):
             hankel[slot, part * ROWS : (part + 1) * ROWS, :] = shifted[:, part * ROWS : part * ROWS + wide]
         matrix = jnp.concatenate(
@@ -91,6 +99,7 @@
         out_shape=jax.ShapeDtypeStruct((out_len // LANES, slots, LANES), jnp.float32),
         scratch_shapes=[
             pltpu.VMEM((group, length), jnp.float32),
+            pltpu.VMEM((group, ROWS, length), jnp.bfloat16),
             pltpu.VMEM((2, LANES, length - LANES), jnp.bfloat16),
             pltpu.VMEM((group, chunk), jnp.float32),
         ],

time: 51.6 us -> 48.2 us (0.934)
  Pallas kernels: 50.1 us -> 46.7 us
    pallas_call x1, Pallas kernels: 27 us -> 23.6 us  [station_sums(): pl.pallas_call(functools.partial(correlate_group, chunk, window), grid=(o...]
where the time goes in v5:
time: 48.2 us; the launch traced here: 47.9 us
  Pallas kernels  46.7 us (97%)
  local copies, waits for them, and re-layouts  1.26 us (3%)
    pallas_call x1, Pallas kernels, station_sums(): pl.pallas_call(functools.partial(correlate_group, chunk, window), grid=(o...  23.6 us
    pallas_call x1, Pallas kernels, collect_stream(): pl.pallas_call(functools.partial(collect_rows, count), in_specs=[pl.Block...  13.6 us
    pallas_call x1, Pallas kernels, reduce_parts(): pl.pallas_call(reduce_blocks, in_specs=[pl.BlockSpec(memory_space=pltpu.V...  9.52 us
    unnamed x1, local copies, waits for them, and re-layouts  1.26 us

profile of v5, /device:TPU:0, one launch (start us, length us, event | category | flops | bytes accessed | tf_op | source)
XLA Modules:
  0.0 47.9 jit_solution(12845479235227695460)
XLA Ops:
  0.0 13.6 %collect_stream.1 = (f32[128,1280]{1,0:T(8,128)}, f32[2,2048,128]{2,1,0:T(8,128)}, f32[16,128]{1,0:T(8,128)}) custom-call(s32[2,8]{1,0:T(2,128)} %ids_ref.1, bf16[1024,128]{1,0:T(8,128)(2,1)} %records_ref.1, bf16[1024,255]{1,0:T(8,128)(2,1)} %following_ref.1, bf16[32,128,256]{2,1,0:T(8,128)(2,1)} %library_ref.1, s32[32,2048]{1,0:T(8,128)} %mask_ref.1, ...), custom_call_target="tpu_custom_call" | custom-call | tf_op jit(solution)/shard_map/collect_stream/pallas_call | solution.py:197
  13.6 23.6 %station_sums.1 = f32[8,16,128]{2,1,0:T(8,128)} custom-call(f32[128,1280]{1,0:T(8,128)} %get-tuple-element.8.stream_ref, f32[2,2048,128]{2,1,0:T(8,128)} %get-tuple-element.9.temps_ref, f32[16,128]{1,0:T(8,128)} %get-tuple-element.10.weights_ref), custom_call_target="tpu_custom_call" | custom-call | tf_op jit(solution)/shard_map/station_sums/pallas_call | solution.py:90
  37.2 9.5 %reduce_parts.1 = f32[8,128]{1,0:T(8,128)} custom-call(f32[8,2,8,128]{3,2,1,0:T(8,128)} %bitcast.3), custom_call_target="tpu_custom_call" | custom-call | tf_op jit(solution)/shard_map/reduce_parts/pallas_call | solution.py:254
  46.7 1.3 %copy.8 = f32[1,8,128]{2,1,0:T(8,128)} copy(f32[1,8,128]{2,1,0:T(8,128)} %bitcast.4) | data formatting | bytes 8192

commit v6 on v5

--- a/solution.py
+++ b/solution.py
@@ -21,16 +21,6 @@
     start = pl.multiple_of(pl.program_id(0) * chunk, LANES)
     rows = stream_ref[:, pl.ds(start, length)]
 
-    total = rows * rows
-    span = 1
-    while span < LANES:
-        total = total + pltpu.roll(total, length - span, 1)
-        span *= 2
-    energy = total[:, :chunk]
-    for step in range(1, window // LANES):
-        energy = energy + total[:, step * LANES : step * LANES + chunk]
-    scale[...] = lax.rsqrt(energy / window + epsilon)
-
     ahead[...] = pltpu.roll(rows, length - (ROWS - 1), 1)
     batch = min(8, group)
 
@@ -42,6 +32,21 @@
         return carry
 
     lax.fori_loop(0, group // batch, turn_rows, 0)
+
+    square = rows * rows
+    high = square.astype(jnp.bfloat16)
+    low = (square - high.astype(jnp.float32)).astype(jnp.bfloat16)
+    depth = window + LANES
+    late = lax.broadcasted_iota(jnp.int32, (depth, LANES), 0) - lax.broadcasted_iota(jnp.int32, (depth, LANES), 1)
+    band = jnp.logical_and(late >= 0, late < window).astype(jnp.float32).astype(jnp.bfloat16)
+    frames = [
+        half[:, block * LANES : block * LANES + depth] for half in (high, low) for block in range(chunk // LANES)
+    ]
+    sums = jnp.dot(jnp.concatenate(frames, axis=0), band, preferred_element_type=jnp.float32)
+    sums = sums[: sums.shape[0] // 2] + sums[sums.shape[0] // 2 :]
+    for block in range(chunk // LANES):
+        energy = sums[block * group : (block + 1) * group] / window
+        scale[:, block * LANES : (block + 1) * LANES] = lax.rsqrt(energy + epsilon)
 
     wide = length - LANES
     slots, lanes = weights_ref.shape

time: 48.2 us -> 44.8 us (0.929)
  Pallas kernels: 46.7 us -> 43.3 us
    pallas_call x1, Pallas kernels: 23.6 us -> 20.2 us  [station_sums(): pl.pallas_call(functools.partial(correlate_group, chunk, window), grid=(o...]
where the time goes in v6:
time: 44.8 us; the launch traced here: 44.5 us
  Pallas kernels  43.3 us (97%)
  local copies, waits for them, and re-layouts  1.26 us (3%)
    pallas_call x1, Pallas kernels, station_sums(): pl.pallas_call(functools.partial(correlate_group, chunk, window), grid=(o...  20.2 us
    pallas_call x1, Pallas kernels, collect_stream(): pl.pallas_call(functools.partial(collect_rows, count), in_specs=[pl.Block...  13.6 us
    pallas_call x1, Pallas kernels, reduce_parts(): pl.pallas_call(reduce_blocks, in_specs=[pl.BlockSpec(memory_space=pltpu.V...  9.51 us
    unnamed x1, local copies, waits for them, and re-layouts  1.26 us

profile of v6, /device:TPU:0, one launch (start us, length us, event | category | flops | bytes accessed | tf_op | source)
XLA Modules:
  0.0 44.5 jit_solution(14665490295617732954)
XLA Ops:
  0.0 13.6 %collect_stream.1 = (f32[128,1280]{1,0:T(8,128)}, f32[2,2048,128]{2,1,0:T(8,128)}, f32[16,128]{1,0:T(8,128)}) custom-call(s32[2,8]{1,0:T(2,128)} %ids_ref.1, bf16[1024,128]{1,0:T(8,128)(2,1)} %records_ref.1, bf16[1024,255]{1,0:T(8,128)(2,1)} %following_ref.1, bf16[32,128,256]{2,1,0:T(8,128)(2,1)} %library_ref.1, s32[32,2048]{1,0:T(8,128)} %mask_ref.1, ...), custom_call_target="tpu_custom_call" | custom-call | tf_op jit(solution)/shard_map/collect_stream/pallas_call | solution.py:202
  13.6 20.2 %station_sums.1 = f32[8,16,128]{2,1,0:T(8,128)} custom-call(f32[128,1280]{1,0:T(8,128)} %get-tuple-element.8.stream_ref, f32[2,2048,128]{2,1,0:T(8,128)} %get-tuple-element.9.temps_ref, f32[16,128]{1,0:T(8,128)} %get-tuple-element.10.weights_ref), custom_call_target="tpu_custom_call" | custom-call | tf_op jit(solution)/shard_map/station_sums/pallas_call | solution.py:95
  33.8 9.5 %reduce_parts.1 = f32[8,128]{1,0:T(8,128)} custom-call(f32[8,2,8,128]{3,2,1,0:T(8,128)} %bitcast.3), custom_call_target="tpu_custom_call" | custom-call | tf_op jit(solution)/shard_map/reduce_parts/pallas_call | solution.py:259
  43.3 1.3 %copy.8 = f32[1,8,128]{2,1,0:T(8,128)} copy(f32[1,8,128]{2,1,0:T(8,128)} %bitcast.4) | data formatting | bytes 8192

commit v7 on v6

--- a/solution.py
+++ b/solution.py
@@ -87,7 +87,7 @@
     stations = stream.shape[0]
     slots, lanes = weights.shape
     window = temps.shape[0] * LANES
-    group = min(16, stations)
+    group = min(32, stations)
     chunk = min(1024, out_len)
     length = chunk + window
     full = stream.shape[1]

time: 44.8 us -> 43.9 us (0.980)
  Pallas kernels: 43.3 us -> 42.4 us
    pallas_call x1, Pallas kernels: 20.2 us -> 19.3 us  [station_sums(): pl.pallas_call(functools.partial(correlate_group, chunk, window), grid=(o...]
where the time goes in v7:
time: 43.9 us; the launch traced here: 43.6 us
  Pallas kernels  42.4 us (97%)
  local copies, waits for them, and re-layouts  1.26 us (3%)
    pallas_call x1, Pallas kernels, station_sums(): pl.pallas_call(functools.partial(correlate_group, chunk, window), grid=(o...  19.3 us
    pallas_call x1, Pallas kernels, collect_stream(): pl.pallas_call(functools.partial(collect_rows, count), in_specs=[pl.Block...  13.6 us
    pallas_call x1, Pallas kernels, reduce_parts(): pl.pallas_call(reduce_blocks, in_specs=[pl.BlockSpec(memory_space=pltpu.V...  9.51 us
    unnamed x1, local copies, waits for them, and re-layouts  1.26 us

profile of v7, /device:TPU:0, one launch (start us, length us, event | category | flops | bytes accessed | tf_op | source)
XLA Modules:
  0.0 43.6 jit_solution(12868280077016684649)
XLA Ops:
  0.0 13.6 %collect_stream.1 = (f32[128,1280]{1,0:T(8,128)}, f32[2,2048,128]{2,1,0:T(8,128)}, f32[16,128]{1,0:T(8,128)}) custom-call(s32[2,8]{1,0:T(2,128)} %ids_ref.1, bf16[1024,128]{1,0:T(8,128)(2,1)} %records_ref.1, bf16[1024,255]{1,0:T(8,128)(2,1)} %following_ref.1, bf16[32,128,256]{2,1,0:T(8,128)(2,1)} %library_ref.1, s32[32,2048]{1,0:T(8,128)} %mask_ref.1, ...), custom_call_target="tpu_custom_call" | custom-call | tf_op jit(solution)/shard_map/collect_stream/pallas_call | solution.py:202
  13.6 19.3 %station_sums.1 = f32[8,16,128]{2,1,0:T(8,128)} custom-call(f32[128,1280]{1,0:T(8,128)} %get-tuple-element.8.stream_ref, f32[2,2048,128]{2,1,0:T(8,128)} %get-tuple-element.9.temps_ref, f32[16,128]{1,0:T(8,128)} %get-tuple-element.10.weights_ref), custom_call_target="tpu_custom_call" | custom-call | tf_op jit(solution)/shard_map/station_sums/pallas_call | solution.py:95
  32.9 9.5 %reduce_parts.1 = f32[8,128]{1,0:T(8,128)} custom-call(f32[8,2,8,128]{3,2,1,0:T(8,128)} %bitcast.3), custom_call_target="tpu_custom_call" | custom-call | tf_op jit(solution)/shard_map/reduce_parts/pallas_call | solution.py:259
  42.4 1.3 %copy.8 = f32[1,8,128]{2,1,0:T(8,128)} copy(f32[1,8,128]{2,1,0:T(8,128)} %bitcast.4) | data formatting | bytes 8192
